TPU v7x, 512 devices: a whole 4x4x16 slice. The times are simulated.
512 devices in a mesh: tm: 16 (over z_hi, y), pipe: 2 (over core), dp: 16 (over x, z_lo).
Axes of the slice: x: 4, y: 4, z: 16 (z_hi: 4, z_lo: 4; z = z_hi * 4 + z_lo), core: 2. Of those that a mesh axis runs over, the one named last changes fastest.
Arguments:
- resid_in: float32 [2, 96, 1024, 1408], P('pipe', 'dp', 'tm'), may hold values from -6 to 6
- ln_gain: float32 [2, 1408], P('pipe'), may hold values from 0.5 to 1.5
- ln_bias: float32 [2, 1408], P('pipe'), may hold values from -2 to 2
- qkv_weight: bfloat16 [2, 1408, 2112], P('pipe', None, 'dp'), may hold values from -0.15625 to 0.15625
- q_bias: float32 [2, 704], P('pipe'), may hold values from -3 to 3
- v_bias: float32 [2, 704], P('pipe'), may hold values from -3 to 3
- out_weight: bfloat16 [2, 1408, 704], P('pipe', None, 'dp'), may hold values from -0.21875 to 0.21875
- out_bias: float32 [2, 1408], P('pipe'), may hold values from -2 to 2
- pattern: int32 [16, 96, 2], P('tm', 'dp'), may hold values from 0 to 14, all different within a row; in each aligned block of 6 rows (0 to 5, 6 to 11, ..., all dimensions but the last counted through in order) at most 2 rows name the same one
- drop_flags: int32 [2, 96], P('pipe', 'dp'), may hold values 0 or 1
Outputs:
- handoff: float32 [2, 96, 1024, 1408], P('pipe', 'dp', 'tm')
Inputs may be any that keep to these rules, and one draw needn't show every extreme that they name: `pattern`: offset v of query block b names key block (b + 1 + v) mod 16; the 2 offsets of one query block and clip differ. Among the 6 clips of one dp index, one query block names one key block in at most 2 clips. `drop_flags`: 1 marks a layer dropped for a clip.
All inputs are finite; a program needn't handle non-finite values. No bound on the sum of `drop_flags` on one device may be relied on, other than what follows from the above.
Results may differ from a plain program's by a relative error of at most 0.0019.
Values may be sent and summed in bfloat16 or wider, within the bound.
No kernel may reach another device: no remote copies, remote signals or barrier semaphores. Data moves between devices by JAX's collectives and lax.ppermute only.
A program may use at most 64 MiB of HBM per device.

v0:
```python
import jax
import jax.numpy as jnp
from jax import lax
from jax.sharding import PartitionSpec as P

HEAD_DIM = 88
drop_rate = 0.25


def from_behind(x, axis, by):
    count = lax.axis_size(axis)
    return lax.ppermute(x, axis, [(i, (i + by) % count) for i in range(count)])


def body(
    resid_in,
    ln_gain,
    ln_bias,
    qkv_weight,
    q_bias,
    v_bias,
    out_weight,
    out_bias,
    pattern,
    drop_flags,
):
    clip_count = resid_in.shape[1]
    block_len = resid_in.shape[2]
    model_width = resid_in.shape[3]
    hidden = q_bias.shape[1]
    head_dim = HEAD_DIM
    head_count = hidden // head_dim
    listed_count = pattern.shape[2]
    tm_size = lax.axis_size("tm")
    my_block = lax.axis_index("tm")
    row_count = clip_count * block_len
    residual = resid_in[0].reshape(row_count, model_width)
    average = jnp.mean(residual, axis=1, keepdims=True)
    centred = residual - average
    spread = jnp.mean(centred * centred, axis=1, keepdims=True)
    normed = (centred * lax.rsqrt(spread + 1e-06) * ln_gain[0] + ln_bias[0]).astype(jnp.bfloat16)
    bias_full = jnp.concatenate([q_bias[0], jnp.zeros((hidden,), jnp.float32), v_bias[0]])
    projected_wide = jnp.dot(
        normed,
        lax.all_gather(qkv_weight[0], "dp", axis=1, tiled=True),
        preferred_element_type=jnp.float32,
    )
    projected = (projected_wide + bias_full).astype(jnp.bfloat16)
    queries = projected[:, :hidden].reshape(clip_count, block_len, head_count, head_dim)
    kv_local = projected[:, hidden:].reshape(clip_count, block_len, 2 * hidden)
    whole_pattern = lax.all_gather(pattern, "tm", axis=0, tiled=True)
    block_ids = jnp.arange(tm_size, dtype=jnp.int32)
    targets = (block_ids[:, None, None] + 1 + whole_pattern) % tm_size
    listed = jnp.sum((targets[..., None] == block_ids).astype(jnp.int32), axis=2)
    rank_table = jnp.cumsum(listed, axis=1) - listed
    capacity = max(2, (clip_count * listed_count + tm_size - 3) // (tm_size - 1))
    slot_ids = jnp.arange(capacity, dtype=jnp.int32)
    listed_mine = lax.dynamic_index_in_dim(listed, my_block, 2, keepdims=False)
    ranks_mine = lax.dynamic_index_in_dim(rank_table, my_block, 2, keepdims=False)
    selection = (
        (listed_mine[:, None, :] == 1) & (ranks_mine[:, None, :] == slot_ids[None, :, None])
    ).astype(jnp.bfloat16)
    outgoing = jnp.einsum(
        "qjc,cre->qjre", selection, kv_local, preferred_element_type=jnp.float32
    ).astype(jnp.bfloat16)
    incoming = lax.all_to_all(outgoing, "tm", split_axis=0, concat_axis=0, tiled=True)
    my_targets = lax.dynamic_index_in_dim(targets, my_block, 0, keepdims=False)
    my_ranks = lax.dynamic_index_in_dim(rank_table, my_block, 0, keepdims=False)
    slot_of = jnp.take_along_axis(my_ranks, my_targets, axis=1)
    flat_index = my_targets * capacity + slot_of
    remote = incoming.reshape(tm_size * capacity, block_len, 2 * hidden)[flat_index]
    gathered = jnp.concatenate([kv_local[:, None], remote], axis=1)
    gathered = gathered.reshape(clip_count, (1 + listed_count) * block_len, 2 * hidden)
    near_keys = gathered[..., :hidden].reshape(
        clip_count, (1 + listed_count) * block_len, head_count, head_dim
    )
    near_vals = gathered[..., hidden:].reshape(
        clip_count, (1 + listed_count) * block_len, head_count, head_dim
    )
    scores = jnp.einsum(
        "cqhd,ckhd->chqk", queries, near_keys, preferred_element_type=jnp.float32
    ) * head_dim ** (-0.5)
    weights = jnp.exp(scores)
    totals = jnp.sum(weights, axis=3)
    weighted = jnp.einsum(
        "chqk,ckhd->cqhd",
        weights.astype(jnp.bfloat16),
        near_vals,
        preferred_element_type=jnp.float32,
    )
    attended = (weighted / jnp.transpose(totals, (0, 2, 1))[..., None]).astype(jnp.bfloat16)
    attended = attended.reshape(row_count, hidden)
    branch = lax.dot_general(
        attended,
        lax.all_gather(out_weight[0], "dp", axis=1, tiled=True),
        (((1,), (1,)), ((), ())),
        preferred_element_type=jnp.float32,
    )
    branch = branch + out_bias[0]
    survive = (1 - drop_flags[0]).astype(jnp.float32)
    updated = residual.reshape(clip_count, block_len, model_width) + survive[
        :, None, None
    ] * branch.reshape(clip_count, block_len, model_width) / (1.0 - drop_rate)
    received = from_behind(updated, "pipe", 1)
    return received[None]


def solution(mesh):
    return jax.shard_map(
        body,
        mesh=mesh,
        in_specs=(
            P("pipe", "dp", "tm", None),
            P("pipe", None),
            P("pipe", None),
            P("pipe", None, "dp"),
            P("pipe", None),
            P("pipe", None),
            P("pipe", None, "dp"),
            P("pipe", None),
            P("tm", "dp", None),
            P("pipe", "dp"),
        ),
        out_specs=P("pipe", "dp", "tm", None),
        check_vma=False,
    )
```

profile of v0, /device:TPU:83, one launch (start us, length us, event | category | flops | bytes accessed | tf_op | source)
XLA Modules:
  0.0 681.6 jit_solution(11258215063038829731)
XLA Ops:
  6.5 2.6 copy.84
  9.1 0.7 reduce.3
  9.9 0.7 reduce.2
  10.6 1.8 reduce_sum.36
  12.5 0.3 multiply_reduce_fusion
  13.0 44.7 %all_gather.10 = s32[16,6,2]{1,2,0:T(2,128)S(1)} all-gather(s32[1,6,2]{1,2,0:T(2,128)S(1)} %copy-done.7), channel_id=1, replica_groups=mesh['tm'=16,'pipe'=2,'dp'=16] {'tm'}, dimensions={0}, use_global_device_ids=true | all-gather | bytes 816 | tf_op jit(solution)/shard_map/all_gather | solution.py:51
  57.7 0.1 and_select_fusion
  57.8 0.1 copy.86
  57.9 0.1 concatenate.6
  58.0 0.1 convert_reduce_fusion
  58.1 0.2 reduce-window_subtract_fusion
  58.3 0.2 dynamic-slice_reduce_fusion
  58.5 0.3 fusion.27
  58.8 0.4 fusion.14
  59.2 214.3 %all-gather.5.cloned.1.call-done = bf16[1,1408,2112]{1,0,2:T(2,128)(2,1)} async-done(((bf16[1,1408,132]{1,0,2:T(2,128)(2,1)}), bf16[1,1408,2112]{1,0,2:T(2,128)(2,1)}) %all-gather.5.cloned.1.call-update) | async-done | bytes 5947408 | tf_op jit(solution)/shard_map/all_gather | solution.py:45
  273.5 7.8 %fusion.6 = bf16[384,2112]{0,1:T(8,128)(2,1)S(1)} fusion(bf16[384,1408]{1,0:T(8,128)(2,1)S(1)} %fusion.14, bf16[1,1408,2112]{1,0,2:T(2,128)(2,1)} %all-gather.5.cloned.1.call-done, f32[2112]{0:T(1024)S(1)} %concatenate.6), kind=kOutput, calls=%fused_computation.7 | convolution fusion | flops 2285420544 | bytes 8659200 | tf_op jit(solution)/shard_map/dot_general | solution.py:43
  281.3 1.1 copy-done.2
  282.4 1.1 slice.20
  283.5 1.7 copy.85
  285.2 2.3 convolution_convert_fusion
  287.6 3.9 copy.89
  291.4 12.0 %all-to-all-start = ((bf16[16,2,64,1408]{3,2,1,0:T(8,128)(2,1)}), bf16[16,2,64,1408]{3,2,1,0:T(8,128)(2,1)}, u32[]{:S(2)}, u32[]{:S(2)}) async-start(bf16[16,2,64,1408]{3,2,1,0:T(8,128)(2,1)} %copy.89), calls=%async_computation | async-start | bytes 11534336 | tf_op jit(solution)/shard_map/all_to_all | solution.py:66
  303.5 0.2 all-gather.7.cloned.1.call-start
  303.7 0.9 copy.99
  304.7 0.1 copy.90
  304.8 0.1 reshape.187
  304.9 0.7 gather_fusion.1
  305.5 0.1 gather.10
  305.6 0.1 copy.91
  305.7 0.1 copy.92
  305.8 0.1 reshape.181
  306.0 1.9 slice.22
  307.9 2.7 reshape.199
  310.6 328.4 %all-to-all-done = bf16[16,2,64,1408]{3,2,1,0:T(8,128)(2,1)} async-done(((bf16[16,2,64,1408]{3,2,1,0:T(8,128)(2,1)}), bf16[16,2,64,1408]{3,2,1,0:T(8,128)(2,1)}, u32[]{:S(2)}, u32[]{:S(2)}) %all-to-all-start) | async-done | bytes 5767200 | tf_op jit(solution)/shard_map/all_to_all | solution.py:66
  639.0 4.9 gather_fusion
  643.9 1.9 pad_maximum_fusion
  645.8 2.6 fusion.36
  648.4 3.9 copy.94
  652.3 4.0 copy.96
  656.3 3.5 fusion.9
  659.8 0.8 fusion.19
  660.6 0.5 copy.98
  661.1 0.6 reshape.177
  661.7 3.2 convolution_add_fusion
  664.9 0.4 bitcast_add_fusion
  665.4 4.2 collective-permute-start
  669.5 3.9 collective-permute-done
  673.4 1.3 copy.129
  (36 shorter events, 0.4 us)
Async XLA Ops:
  6.5 6.0 copy-start
  6.5 266.9 %all-gather.5.cloned.1.call-start = ((), (), s32[]{:S(2)}) async-start(), calls=%async_computation.1 | async-start | bytes 12638208 | tf_op jit(solution)/shard_map/all_gather | solution.py:45
  10.6 2.4 copy-start.5
  10.6 2.4 copy-start.6
  10.6 2.4 copy-start.7
  281.3 1.2 copy-start.2
  291.4 12.3 %copy-start.3 = (bf16[1,1408,44]{1,2,0:T(8,128)(2,1)S(1)}, bf16[1,1408,44]{1,2,0:T(8,128)(2,1)}, u32[]{:S(2)}) copy-start(bf16[1,1408,44]{1,2,0:T(8,128)(2,1)} %param.16) | copy-start | bytes 371716
  291.4 347.6 %all-to-all-start = ((bf16[16,2,64,1408]{3,2,1,0:T(8,128)(2,1)}), bf16[16,2,64,1408]{3,2,1,0:T(8,128)(2,1)}, u32[]{:S(2)}, u32[]{:S(2)}) async-start(bf16[16,2,64,1408]{3,2,1,0:T(8,128)(2,1)} %copy.89), calls=%async_computation | async-start | bytes 11534336 | tf_op jit(solution)/shard_map/all_to_all | solution.py:66
  303.5 358.2 %all-gather.7.cloned.1.call-start = ((), (), s32[]{:S(2)}) async-start(), calls=%async_computation.2 | async-start | bytes 4212736 | tf_op jit(solution)/shard_map/all_gather | solution.py:95
  304.6 1.3 copy-start.4
  304.6 1.3 copy-start.8
  656.3 3.5 copy-start.1
  665.4 8.0 %collective-permute-start = (f32[6,64,1408]{2,1,0:T(8,128)S(1)}, f32[6,64,1408]{2,1,0:T(8,128)S(1)}, u32[]{:S(2)}, u32[]{:S(2)}) collective-permute-start(f32[6,64,1408]{2,1,0:T(8,128)S(1)} %bitcast_add_fusion), channel_id=1, source_target_pairs={{0,16},{16,0},{1,17},{17,1},{2,18},{18,2},{3,19},{19,3},{4,20},{20... | collective-permute-start | bytes 6488072 | tf_op jit(solution)/shard_map/ppermute | solution.py:12
Sparse Core Ops, SparseCore 0:
  9.4 264.0 all-gather.4
  306.4 311.5 all-gather.6
where the time goes:
time: 682 us
  waiting for transfers between devices  547 us (80%)
  blocking collectives  44.7 us (7%)
  local copies, waits for them, and re-layouts  35.5 us (5%)
  matrix products  17.6 us (3%)
  starting transfers between devices  16.4 us (2%)
  between operations  13.7 us (2%)
  other arithmetic  7.06 us (1%)
    all_to_all x1, waiting for transfers between devices, body(): lax.all_to_all(outgoing, 'tm', split_axis=0, concat_axis=0, tiled=True)  328 us
    all_gather x1, waiting for transfers between devices, body(): lax.all_gather(qkv_weight[0], 'dp', axis=1, tiled=True)  214 us
    all_gather x1, blocking collectives, body(): whole_pattern = lax.all_gather(pattern, 'tm', axis=0, tiled=True)  44.7 us
  transfers between devices with their start and end apart: 4, of which 3 were waited for; matrix products, arithmetic and copies ran while one was open for 5% of the time, Pallas kernels for 0%

commit v1 on v0

--- a/solution.py
+++ b/solution.py
@@ -1,3 +1,4 @@
+import functools
 import jax
 import jax.numpy as jnp
 from jax import lax
@@ -5,6 +6,16 @@
 
 HEAD_DIM = 88
 drop_rate = 0.25
+
+
+def apply_the_corner(raw, bus_axis):
+    chunks = []
+    for _ in range(lax.axis_size(bus_axis)):
+        chunks.append(raw)
+    return jnp.concatenate(lax.all_to_all(jnp.stack(chunks, axis=0), bus_axis, 0, 0), 1)
+
+
+open_tiles_in = functools.partial(apply_the_corner, bus_axis="dp")
 
 
 def from_behind(x, axis, by):
@@ -41,9 +52,7 @@
     normed = (centred * lax.rsqrt(spread + 1e-06) * ln_gain[0] + ln_bias[0]).astype(jnp.bfloat16)
     bias_full = jnp.concatenate([q_bias[0], jnp.zeros((hidden,), jnp.float32), v_bias[0]])
     projected_wide = jnp.dot(
-        normed,
-        lax.all_gather(qkv_weight[0], "dp", axis=1, tiled=True),
-        preferred_element_type=jnp.float32,
+        normed, open_tiles_in(qkv_weight[0]), preferred_element_type=jnp.float32
     )
     projected = (projected_wide + bias_full).astype(jnp.bfloat16)
     queries = projected[:, :hidden].reshape(clip_count, block_len, head_count, head_dim)

time: 682 us -> 573 us (0.84)
  waiting for transfers between devices: 547 us -> 301 us
  blocking collectives: 44.7 us -> 165 us
  starting transfers between devices: 16.4 us -> 27.4 us
  local copies, waits for them, and re-layouts: 35.5 us -> 44.9 us
    all_gather x1 -> x0, waiting for transfers between devices: 214 us -> none  [body(): lax.all_gather(qkv_weight[0], 'dp', axis=1, tiled=True)]
    all_gather x1, blocking collectives: 44.7 us -> 165 us  [body(): whole_pattern = lax.all_gather(pattern, 'tm', axis=0, tiled=True)]
    all_to_all x1, waiting for transfers between devices: 328 us -> 297 us  [body(): lax.all_to_all(outgoing, 'tm', split_axis=0, concat_axis=0, tiled=True)]
    reshape x0 -> x1, local copies, waits for them, and re-layouts: none -> 8.07 us  [apply_the_corner(): jnp.concatenate(lax.all_to_all(jnp.stack(chunks, axis=0), bus_axis, 0, 0)...]
    all_to_all x0 -> x1, starting transfers between devices: none -> 7.58 us  [apply_the_corner(): lax.all_to_all(jnp.stack(chunks, axis=0), bus_axis, 0, 0)]
  transfers between devices with their start and end apart: 4 -> 4, of which waited for: 3 -> 2; matrix products, arithmetic and copies ran while one was open for 5% -> 6% of each run, Pallas kernels for 0% -> 0%
where the time goes in v1:
time: 573 us; the launch traced here: 572 us
  waiting for transfers between devices  301 us (53%)
  blocking collectives  165 us (29%)
  local copies, waits for them, and re-layouts  44.9 us (8%)
  starting transfers between devices  27.4 us (5%)
  matrix products  15.9 us (3%)
  between operations  13.7 us (2%)
    all_to_all x1, waiting for transfers between devices, body(): lax.all_to_all(outgoing, 'tm', split_axis=0, concat_axis=0, tiled=True)  297 us
    all_gather x1, blocking collectives, body(): whole_pattern = lax.all_gather(pattern, 'tm', axis=0, tiled=True)  165 us
    all_to_all x1, starting transfers between devices, body(): lax.all_to_all(outgoing, 'tm', split_axis=0, concat_axis=0, tiled=True)  17.2 us
  transfers between devices with their start and end apart: 4, of which 2 were waited for; matrix products, arithmetic and copies ran while one was open for 6% of the time, Pallas kernels for 0%

profile of v1, /device:TPU:83, one launch (start us, length us, event | category | flops | bytes accessed | tf_op | source)
XLA Modules:
  0.0 572.3 jit_solution(12624082161876811554)
XLA Ops:
  6.5 4.0 stack.3
  10.6 7.6 %all-to-all-start = ((bf16[16,1408,132]{1,2,0:T(8,128)(2,1)}), bf16[16,1408,132]{1,2,0:T(8,128)(2,1)}, u32[]{:S(2)}, u32[]{:S(2)}) async-start(bf16[16,1408,132]{1,2,0:T(8,128)(2,1)} %stack.3), calls=%async_computation | async-start | bytes 12255232 | tf_op jit(solution)/shard_map/all_to_all | solution.py:15
  18.2 165.1 %all_gather.6 = s32[16,6,2]{1,2,0:T(2,128)S(1)} all-gather(s32[1,6,2]{1,2,0:T(2,128)S(1)} %copy-done.9), channel_id=1, replica_groups=mesh['tm'=16,'pipe'=2,'dp'=16] {'tm'}, dimensions={0}, use_global_device_ids=true | all-gather | bytes 816 | tf_op jit(solution)/shard_map/all_gather | solution.py:60
  183.3 0.1 and_select_fusion
  183.4 0.1 copy.83
  183.7 0.2 reduce_sum.36
  183.9 0.1 concatenate.6
  183.9 0.1 convert_reduce_fusion
  184.0 0.2 reduce-window_subtract_fusion
  184.2 0.2 dynamic-slice_reduce_fusion
  184.4 0.3 fusion.15
  184.7 0.3 multiply_reduce_fusion
  185.1 0.4 add_convert_fusion
  185.5 8.1 %reshape.195 = bf16[1408,2112]{0,1:T(8,128)(2,1)} reshape(bf16[1408,16,132]{0,2,1:T(8,128)(2,1)} %bitcast.4) | data formatting | bytes 11894784 | tf_op jit(solution)/shard_map/reshape | solution.py:15
  193.6 6.1 %fusion = bf16[384,2112]{0,1:T(8,128)(2,1)S(1)} fusion(bf16[384,1408]{1,0:T(8,128)(2,1)S(1)} %bitcast.73, bf16[1408,2112]{0,1:T(8,128)(2,1)} %reshape.195, f32[2112]{0:T(1024)S(1)} %concatenate.6), kind=kOutput, calls=%fused_computation.4 | convolution fusion | flops 2285420544 | bytes 8659200 | tf_op jit(solution)/shard_map/dot_general | solution.py:54
  199.7 1.1 copy-done.2
  200.9 1.1 slice.20
  202.0 1.7 copy.82
  203.7 2.3 convolution_convert_fusion
  206.0 3.9 copy.86
  209.9 17.2 %all-to-all-start.1 = ((bf16[16,2,64,1408]{3,2,1,0:T(8,128)(2,1)}), bf16[16,2,64,1408]{3,2,1,0:T(8,128)(2,1)}, u32[]{:S(2)}, u32[]{:S(2)}) async-start(bf16[16,2,64,1408]{3,2,1,0:T(8,128)(2,1)} %copy.86), calls=%async_computation.1 | async-start | bytes 11534336 | tf_op jit(solution)/shard_map/all_to_all | solution.py:75
  227.0 0.2 all-gather.3.cloned.1.call-start
  227.3 0.9 copy.96
  228.2 0.1 copy.87
  228.3 0.1 reshape.212
  228.4 0.7 gather_fusion.1
  229.1 0.1 gather.10
  229.2 0.1 copy.88
  229.3 0.1 copy.89
  229.4 0.1 reshape.206
  229.5 1.9 slice.22
  231.5 2.7 reshape.223
  234.1 297.3 %all-to-all-done.1 = bf16[16,2,64,1408]{3,2,1,0:T(8,128)(2,1)} async-done(((bf16[16,2,64,1408]{3,2,1,0:T(8,128)(2,1)}), bf16[16,2,64,1408]{3,2,1,0:T(8,128)(2,1)}, u32[]{:S(2)}, u32[]{:S(2)}) %all-to-all-start.1) | async-done | bytes 5767200 | tf_op jit(solution)/shard_map/all_to_all | solution.py:75
  531.4 4.9 gather_fusion
  536.3 1.9 pad_maximum_fusion
  538.2 2.6 fusion.24
  540.9 4.0 copy.93
  544.8 3.9 copy.91
  548.8 3.5 fusion.1
  552.3 0.8 fusion.7
  553.0 0.5 copy.95
  553.6 0.6 reshape.202
  554.1 0.0 all-gather.3.cloned.1.call-done
  554.2 3.2 convolution_add_fusion.1
  557.4 0.4 bitcast_add_fusion
  557.8 2.5 collective-permute-start
  560.3 3.9 collective-permute-done
  564.1 1.3 copy.117
  (38 shorter events, 0.2 us)
Async XLA Ops:
  10.6 7.6 %copy-start.9 = (s32[1,6,2]{1,2,0:T(2,128)S(1)}, s32[1,6,2]{1,2,0:T(2,128)}, u32[]{:S(2)}) copy-start(s32[1,6,2]{1,2,0:T(2,128)} %param.18) | copy-start | bytes 148
  10.6 173.0 %copy-start.4 = (f32[1,1408]{1,0:T(1,128)S(1)}, f32[1,1408]{1,0:T(1,128)}, u32[]{:S(2)}) copy-start(f32[1,1408]{1,0:T(1,128)} %param.11) | copy-start | bytes 16900
  10.6 173.0 %copy-start.5 = (f32[1,1408]{1,0:T(1,128)S(1)}, f32[1,1408]{1,0:T(1,128)}, u32[]{:S(2)}) copy-start(f32[1,1408]{1,0:T(1,128)} %param.12) | copy-start | bytes 16900
  10.6 173.0 %copy-start.7 = (f32[1,704]{1,0:T(1,128)S(1)}, f32[1,704]{1,0:T(1,128)}, u32[]{:S(2)}) copy-start(f32[1,704]{1,0:T(1,128)} %param.14) | copy-start | bytes 8452
  10.6 173.1 %copy-start.8 = (f32[1,704]{1,0:T(1,128)S(1)}, f32[1,704]{1,0:T(1,128)}, u32[]{:S(2)}) copy-start(f32[1,704]{1,0:T(1,128)} %param.15) | copy-start | bytes 8452
  10.6 173.1 %copy-start = (f32[1,6,64,1408]{3,2,1,0:T(8,128)S(1)}, f32[1,6,64,1408]{3,2,1,0:T(8,128)}, u32[]{:S(2)}) copy-start(f32[1,6,64,1408]{3,2,1,0:T(8,128)} %param.10) | copy-start | bytes 6488068
  10.6 174.9 %all-to-all-start = ((bf16[16,1408,132]{1,2,0:T(8,128)(2,1)}), bf16[16,1408,132]{1,2,0:T(8,128)(2,1)}, u32[]{:S(2)}, u32[]{:S(2)}) async-start(bf16[16,1408,132]{1,2,0:T(8,128)(2,1)} %stack.3), calls=%async_computation | async-start | bytes 12255232 | tf_op jit(solution)/shard_map/all_to_all | solution.py:15
  199.7 1.2 copy-start.2
  209.9 17.4 %copy-start.3 = (bf16[1,1408,44]{1,2,0:T(8,128)(2,1)S(1)}, bf16[1,1408,44]{1,2,0:T(8,128)(2,1)}, u32[]{:S(2)}) copy-start(bf16[1,1408,44]{1,2,0:T(8,128)(2,1)} %param.16) | copy-start | bytes 371716
  209.9 321.6 %all-to-all-start.1 = ((bf16[16,2,64,1408]{3,2,1,0:T(8,128)(2,1)}), bf16[16,2,64,1408]{3,2,1,0:T(8,128)(2,1)}, u32[]{:S(2)}, u32[]{:S(2)}) async-start(bf16[16,2,64,1408]{3,2,1,0:T(8,128)(2,1)} %copy.86), calls=%async_computation.1 | async-start | bytes 11534336 | tf_op jit(solution)/shard_map/all_to_all | solution.py:75
  227.0 327.1 %all-gather.3.cloned.1.call-start = ((), (), s32[]{:S(2)}) async-start(), calls=%async_computation.2 | async-start | bytes 4212736 | tf_op jit(solution)/shard_map/all_gather | solution.py:104
  228.2 1.3 copy-start.6
  228.2 1.3 copy-start.10
  548.8 3.5 copy-start.1
  557.8 6.3 %collective-permute-start = (f32[6,64,1408]{2,1,0:T(8,128)S(1)}, f32[6,64,1408]{2,1,0:T(8,128)S(1)}, u32[]{:S(2)}, u32[]{:S(2)}) collective-permute-start(f32[6,64,1408]{2,1,0:T(8,128)S(1)} %bitcast_add_fusion), channel_id=1, source_target_pairs={{0,16},{16,0},{1,17},{17,1},{2,18},{18,2},{3,19},{19,3},{4,20},{20... | collective-permute-start | bytes 6488072 | tf_op jit(solution)/shard_map/ppermute | solution.py:23
Sparse Core Ops, SparseCore 0:
  229.9 263.1 all-gather.2
